TPU v7x, 32 devices: a whole 2x2x4 slice. The times are simulated.
32 devices in a mesh: dp: 8 (over y, x, core), tensor: 4 (over z).
Axes of the slice: x: 2, y: 2, z: 4, core: 2. Of those that a mesh axis runs over, the one named last changes fastest.
Arguments:
- inputs: bfloat16 [64, 256, 1152], P('dp'), may hold values from -6 to 6
- cotangent: bfloat16 [64, 256, 1152], P('dp'), may hold values from -6 to 6
- counts: int32 [8], P('dp'), may hold values from 1 to 8, as said below
- time_ids: int32 [64], P('dp'), may hold values from 0 to 999
- class_ids: int32 [64], P('dp'), may hold values from 0 to 1000
- time_table: bfloat16 [1000, 1152], replicated, may hold values from -4 to 4
- class_table: bfloat16 [1001, 1152], replicated, may hold values from -4 to 4
- ada_weight: bfloat16 [1152, 6, 1152], P(None, None, 'tensor'), may hold values from -0.1875 to 0.1875
- ada_bias: bfloat16 [6, 1152], P(None, 'tensor'), may hold values from -1.75 to 1.75
- qkv_weight: bfloat16 [1152, 3, 1152], P(None, None, 'tensor'), may hold values from -0.1875 to 0.1875
- qv_bias: bfloat16 [2, 1152], P(None, 'tensor'), may hold values from -1.75 to 1.75
- proj_weight: bfloat16 [1152, 1152], P('tensor'), may hold values from -1.5 to 1.5
- proj_bias: bfloat16 [1152], replicated, may hold values from -1.75 to 1.75
- up_weight: bfloat16 [1152, 4608], P(None, 'tensor'), may hold values from -0.1875 to 0.1875
- up_bias: bfloat16 [4608], P('tensor'), may hold values from -1.75 to 1.75
- down_weight: bfloat16 [4608, 1152], P('tensor'), may hold values from -0.09375 to 0.09375
- down_bias: bfloat16 [1152], replicated, may hold values from -1.75 to 1.75
Outputs:
- outputs: bfloat16 [64, 256, 1152], P('dp')
- grad_inputs: bfloat16 [64, 256, 1152], P('dp')
- grad_time_table: float32 [1000, 1152], replicated
- grad_class_table: float32 [1001, 1152], replicated
- grad_ada_weight: float32 [1152, 6, 1152], P(None, None, 'tensor')
- grad_ada_bias: float32 [6, 1152], P(None, 'tensor')
- grad_qkv_weight: float32 [1152, 3, 1152], P(None, None, 'tensor')
- grad_qv_bias: float32 [2, 1152], P(None, 'tensor')
- grad_proj_weight: float32 [1152, 1152], P('tensor')
- grad_proj_bias: float32 [1152], replicated
- grad_up_weight: float32 [1152, 4608], P(None, 'tensor')
- grad_up_bias: float32 [4608], P('tensor')
- grad_down_weight: float32 [4608, 1152], P('tensor')
- grad_down_bias: float32 [1152], replicated
Inputs may be any that keep to these rules, and one draw needn't show every extreme that they name: Each index of dp holds 8 image slots whose first counts live; at least one index has all 8 live.
All inputs are finite; a program needn't handle non-finite values.
Results may differ from a plain program's by a relative error of at most 0.014.
The roundings to bfloat16 on the way count: a program that leaves them out, or rounds other values in their place, can miss the bound.
Values sent between devices are 32-bit elements; how exact they have to be, the bound alone decides.
No kernel may reach another device: no remote copies, remote signals or barrier semaphores. Data moves between devices by JAX's collectives and lax.ppermute only.
A program may use at most 256 MiB of HBM per device.

v0:
```python
import jax
import jax.numpy as jnp
from jax import lax
from jax.sharding import PartitionSpec as P

HEAD_DIM = 72
EPSILON = 1e-06
GELU_ROOT = 0.7978845608028654
GELU_CUBIC = 0.044715


def norm_parts(values):
    average = jnp.mean(values, axis=-1, keepdims=True)
    centred = values - average
    spread = jnp.mean(centred * centred, axis=-1, keepdims=True)
    inverse = lax.rsqrt(spread + EPSILON)
    return (centred * inverse, inverse)


def norm_back(upstream, normed, inverse):
    first_mean = jnp.mean(upstream, axis=-1, keepdims=True)
    second_mean = jnp.mean(upstream * normed, axis=-1, keepdims=True)
    return inverse * (upstream - first_mean - normed * second_mean)


def gelu_parts(values):
    argument = GELU_ROOT * (values + GELU_CUBIC * values * values * values)
    tangent = jnp.tanh(argument)
    result = 0.5 * values * (1.0 + tangent)
    derivative = 0.5 * (1.0 + tangent) + 0.5 * values * (1.0 - tangent * tangent) * GELU_ROOT * (
        1.0 + 3.0 * GELU_CUBIC * values * values
    )
    return (result, derivative)


def local(
    inputs,
    cotangent,
    counts,
    time_ids,
    class_ids,
    time_table,
    class_table,
    ada_weight,
    ada_bias,
    qkv_weight,
    qv_bias,
    proj_weight,
    proj_bias,
    up_weight,
    up_bias,
    down_weight,
    down_bias,
):
    wide = jnp.float32
    narrow = jnp.bfloat16
    images, length, width = inputs.shape
    local_width = qkv_weight.shape[2]
    heads_here = local_width // HEAD_DIM
    scaling = HEAD_DIM ** (-0.5)
    live = (jnp.arange(images, dtype=jnp.int32) < counts[0]).astype(wide)
    time_levels = jnp.arange(time_table.shape[0], dtype=jnp.int32)
    class_levels = jnp.arange(class_table.shape[0], dtype=jnp.int32)
    time_pick = (time_ids[:, None] == time_levels[None, :]).astype(narrow)
    class_pick = (class_ids[:, None] == class_levels[None, :]).astype(narrow)
    condition = jnp.dot(time_pick, time_table, preferred_element_type=wide) + jnp.dot(
        class_pick, class_table, preferred_element_type=wide
    )
    silu_cond = jax.nn.silu(condition).astype(narrow)
    mod_local = jnp.einsum(
        "gd,dke->gke", silu_cond, ada_weight, preferred_element_type=wide
    ) + ada_bias.astype(wide)
    modulation = lax.all_gather(mod_local, "tensor", axis=2, tiled=True)
    shift_attn = modulation[:, 0, None, :]
    scale_attn = modulation[:, 1, None, :]
    gate_attn = modulation[:, 2, None, :]
    shift_mlp = modulation[:, 3, None, :]
    scale_mlp = modulation[:, 4, None, :]
    gate_mlp = modulation[:, 5, None, :]
    input_wide = inputs.astype(wide)
    normed_attn, inverse_attn = norm_parts(input_wide)
    hidden_attn = (normed_attn * (1.0 + scale_attn) + shift_attn).astype(narrow)
    projected = jnp.einsum("gsd,dke->gske", hidden_attn, qkv_weight, preferred_element_type=wide)
    bias_wide = qv_bias.astype(wide)
    shape_heads = (images, length, heads_here, HEAD_DIM)
    query_heads = (projected[:, :, 0] + bias_wide[0]).astype(narrow).reshape(shape_heads)
    key_heads = projected[:, :, 1].astype(narrow).reshape(shape_heads)
    value_heads = (projected[:, :, 2] + bias_wide[1]).astype(narrow).reshape(shape_heads)
    scores = (
        jnp.einsum("gqhe,gkhe->ghqk", query_heads, key_heads, preferred_element_type=wide) * scaling
    )
    highest = jnp.max(scores, axis=-1, keepdims=True)
    exponent = jnp.exp(scores - highest)
    denominator = jnp.sum(exponent, axis=-1, keepdims=True)
    soft_probs = (exponent / denominator).astype(narrow)
    log_total = highest + jnp.log(denominator)
    heads_out = jnp.einsum("ghqk,gkhe->gqhe", soft_probs, value_heads, preferred_element_type=wide)
    heads_out = heads_out.reshape(images, length, local_width).astype(narrow)
    attn_part = jnp.einsum("gse,ed->gsd", heads_out, proj_weight, preferred_element_type=wide)
    attention = lax.psum(attn_part, "tensor") + proj_bias.astype(wide)
    middle = input_wide + gate_attn * attention
    normed_mlp, inverse_mlp = norm_parts(middle)
    hidden_mlp = (normed_mlp * (1.0 + scale_mlp) + shift_mlp).astype(narrow)
    pre_act = jnp.einsum(
        "gsd,df->gsf", hidden_mlp, up_weight, preferred_element_type=wide
    ) + up_bias.astype(wide)
    gelu_value, gelu_slope = gelu_parts(pre_act)
    activated = gelu_value.astype(narrow)
    mlp_part = jnp.einsum("gsf,fd->gsd", activated, down_weight, preferred_element_type=wide)
    branch = lax.psum(mlp_part, "tensor") + down_bias.astype(wide)
    outputs = ((middle + gate_mlp * branch) * live[:, None, None]).astype(narrow)
    grad_out = cotangent.astype(wide) * live[:, None, None]
    d_gate_mlp = jnp.sum(grad_out * branch, axis=1)
    d_branch = (gate_mlp * grad_out).astype(narrow)
    grad_down_bias = jnp.sum(d_branch, axis=(0, 1), dtype=wide)
    grad_down_weight = jnp.einsum("gsf,gsd->fd", activated, d_branch, preferred_element_type=wide)
    d_activated = jnp.einsum("gsd,fd->gsf", d_branch, down_weight, preferred_element_type=wide)
    d_pre = (d_activated * gelu_slope).astype(narrow)
    grad_up_bias = jnp.sum(d_pre, axis=(0, 1), dtype=wide)
    grad_up_weight = jnp.einsum("gsd,gsf->df", hidden_mlp, d_pre, preferred_element_type=wide)
    grad_down_weight, grad_down_bias, grad_up_weight, grad_up_bias = lax.psum(
        (grad_down_weight, grad_down_bias, grad_up_weight, grad_up_bias), "dp"
    )
    d_mlp_part = jnp.einsum("gsf,df->gsd", d_pre, up_weight, preferred_element_type=wide)
    d_hidden_mlp = lax.psum(d_mlp_part, "tensor")
    d_shift_mlp = jnp.sum(d_hidden_mlp, axis=1)
    d_scale_mlp = jnp.sum(d_hidden_mlp * normed_mlp, axis=1)
    d_middle = grad_out + norm_back(d_hidden_mlp * (1.0 + scale_mlp), normed_mlp, inverse_mlp)
    d_gate_attn = jnp.sum(d_middle * attention, axis=1)
    d_attention = (gate_attn * d_middle).astype(narrow)
    grad_proj_bias = jnp.sum(d_attention, axis=(0, 1), dtype=wide)
    grad_proj_weight = jnp.einsum(
        "gse,gsd->ed", heads_out, d_attention, preferred_element_type=wide
    )
    d_heads = jnp.einsum("gsd,ed->gse", d_attention, proj_weight, preferred_element_type=wide)
    d_heads = d_heads.astype(narrow).reshape(shape_heads)
    scores_again = (
        jnp.einsum("gqhe,gkhe->ghqk", query_heads, key_heads, preferred_element_type=wide) * scaling
    )
    probs_again = jnp.exp(scores_again - log_total)
    d_value = jnp.einsum(
        "ghqk,gqhe->gkhe", probs_again.astype(narrow), d_heads, preferred_element_type=wide
    )
    d_value = d_value.astype(narrow)
    d_probs = jnp.einsum("gqhe,gkhe->ghqk", d_heads, value_heads, preferred_element_type=wide)
    row_inner = jnp.sum(probs_again * d_probs, axis=-1, keepdims=True)
    d_scores = (probs_again * (d_probs - row_inner)).astype(narrow)
    d_query = (
        jnp.einsum("ghqk,gkhe->gqhe", d_scores, key_heads, preferred_element_type=wide) * scaling
    ).astype(narrow)
    d_key = (
        jnp.einsum("ghqk,gqhe->gkhe", d_scores, query_heads, preferred_element_type=wide) * scaling
    ).astype(narrow)
    d_projected = jnp.stack([d_query, d_key, d_value], axis=2).reshape(
        images, length, 3, local_width
    )
    grad_qv_bias = jnp.stack(
        [
            jnp.sum(d_query, axis=(0, 1), dtype=wide).reshape(local_width),
            jnp.sum(d_value, axis=(0, 1), dtype=wide).reshape(local_width),
        ],
        axis=0,
    )
    grad_qkv_weight = jnp.einsum(
        "gsd,gske->dke", hidden_attn, d_projected, preferred_element_type=wide
    )
    d_attn_part = jnp.einsum("gske,dke->gsd", d_projected, qkv_weight, preferred_element_type=wide)
    d_hidden_attn = lax.psum(d_attn_part, "tensor")
    d_shift_attn = jnp.sum(d_hidden_attn, axis=1)
    d_scale_attn = jnp.sum(d_hidden_attn * normed_attn, axis=1)
    grad_inputs = (
        d_middle + norm_back(d_hidden_attn * (1.0 + scale_attn), normed_attn, inverse_attn)
    ).astype(narrow)
    d_modulation = jnp.stack(
        [d_shift_attn, d_scale_attn, d_gate_attn, d_shift_mlp, d_scale_mlp, d_gate_mlp], axis=1
    ).astype(narrow)
    start_column = lax.axis_index("tensor") * local_width
    d_mod_local = lax.dynamic_slice_in_dim(d_modulation, start_column, local_width, 2)
    grad_ada_weight = jnp.einsum("gd,gke->dke", silu_cond, d_mod_local, preferred_element_type=wide)
    grad_ada_bias = jnp.sum(d_mod_local, axis=0, dtype=wide)
    (
        grad_qkv_weight,
        grad_qv_bias,
        grad_proj_weight,
        grad_proj_bias,
        grad_ada_weight,
        grad_ada_bias,
    ) = lax.psum(
        (
            grad_qkv_weight,
            grad_qv_bias,
            grad_proj_weight,
            grad_proj_bias,
            grad_ada_weight,
            grad_ada_bias,
        ),
        "dp",
    )
    sigmoid_cond = jax.nn.sigmoid(condition)
    d_condition = jnp.einsum("gke,dke->gd", d_mod_local, ada_weight, preferred_element_type=wide)
    d_condition = d_condition * sigmoid_cond * (1.0 + condition * (1.0 - sigmoid_cond))
    exact = lax.Precision.HIGHEST
    grad_time_table = jnp.dot(time_pick.astype(wide).T, d_condition, precision=exact)
    grad_class_table = jnp.dot(class_pick.astype(wide).T, d_condition, precision=exact)
    grad_time_table, grad_class_table = lax.psum(
        (grad_time_table, grad_class_table), ("dp", "tensor")
    )
    return (
        outputs,
        grad_inputs,
        grad_time_table,
        grad_class_table,
        grad_ada_weight,
        grad_ada_bias,
        grad_qkv_weight,
        grad_qv_bias,
        grad_proj_weight,
        grad_proj_bias,
        grad_up_weight,
        grad_up_bias,
        grad_down_weight,
        grad_down_bias,
    )


def solution(mesh):
    in_specs = (
        P("dp", None, None),
        P("dp", None, None),
        P("dp"),
        P("dp"),
        P("dp"),
        P(),
        P(),
        P(None, None, "tensor"),
        P(None, "tensor"),
        P(None, None, "tensor"),
        P(None, "tensor"),
        P("tensor", None),
        P(),
        P(None, "tensor"),
        P("tensor"),
        P("tensor", None),
        P(),
    )
    out_specs = (
        P("dp", None, None),
        P("dp", None, None),
        P(),
        P(),
        P(None, None, "tensor"),
        P(None, "tensor"),
        P(None, None, "tensor"),
        P(None, "tensor"),
        P("tensor", None),
        P(),
        P(None, "tensor"),
        P("tensor"),
        P("tensor", None),
        P(),
    )
    return jax.shard_map(local, mesh=mesh, in_specs=in_specs, out_specs=out_specs, check_vma=False)
```

profile of v0, /device:TPU:0, one launch (start us, length us, event | category | flops | bytes accessed | tf_op | source)
XLA Modules:
  0.0 2098.7 jit_solution(2705256795855632784)
XLA Ops:
  10.5 4.5 fusion.14
  19.4 91.1 %all_gather.3 = f32[8,6,1152]{1,0,2:T(8,128)} all-gather(f32[8,6,288]{1,0,2:T(8,128)} %copy.58), channel_id=1, replica_groups=mesh['dp'=8,'tensor'=4] {'tensor'}, dimensions={2}, use_global_device_ids=true | all-gather | bytes 276480 | tf_op jit(solution)/shard_map/all_gather | solution.py:73
  110.5 22.1 %fusion.73 = (f32[8,1,1152]{1,0,2:T(8,128)}, f32[8,1,1152]{1,0,2:T(8,128)}, f32[8,1,1152]{1,0,2:T(8,128)}, f32[8,1,1152]{1,0,2:T(8,128)}, f32[8,1,1152]{1,0,2:T(8,128)}, /*index=5*/f32[8,1,1152]{1,0,2:T(8,128)}) fusion(f32[8,6,1152]{1,0,2:T(8,128)} %all_gather.3), kind=kLoop, calls=%fused_computation.140 | loop fusion | bytes 442368 | tf_op jit(solution)/shard_map/slice | solution.py:79
  139.3 7.8 fusion.40
  159.6 5.4 fusion.49
  180.0 310.3 %all-reduce.10.cloned.1.call-done = f32[8,256,1152]{2,1,0:T(8,128)} async-done(((f32[8,256,1152]{2,1,0:T(8,128)}), f32[8,256,1152]{2,1,0:T(8,128)}) %all-reduce.10.cloned.1.call-update) | async-done | bytes 9437200 | tf_op jit(solution)/shard_map/psum | solution.py:100
  490.3 10.4 fusion.71
  500.7 4.9 multiply_reduce_fusion.4
  507.1 9.6 fusion.35
  516.7 12.8 convert_reduce_fusion.2
  531.8 9.6 fusion.33
  542.2 13.1 fusion.31
  555.3 309.9 %all-reduce.12.cloned.1.call-done = f32[8,256,1152]{2,1,0:T(8,128)} async-done(((f32[8,256,1152]{2,1,0:T(8,128)}), f32[8,256,1152]{2,1,0:T(8,128)}) %all-reduce.12.cloned.1.call-update) | async-done | bytes 9437200 | tf_op jit(solution)/shard_map/psum | solution.py:125
  865.2 8.5 multiply_reduce_fusion.1
  874.4 11.4 convert_reduce_fusion.3
  900.4 7.9 convolution_bitcast_fusion.2
  909.1 16.6 convolution_bitcast_fusion
  925.7 611.2 %all-reduce.18.cloned.1.call-done = (f32[8,256,1152]{2,1,0:T(8,128)}, f32[8,256,1152]{2,1,0:T(8,128)}) async-done(((f32[8,256,1152]{2,1,0:T(8,128)}, f32[8,256,1152]{2,1,0:T(8,128)}), (f32[8,256,1152]{2,1,0:T(8,128)}, f32[8,256,1152]{2,1,0:T(8,128)})) %all-reduce.18.cloned.1.call-update) | async-done | bytes 18874384 | tf_op jit(solution)/shard_map/psum | solution.py:110
  1537.0 8.8 fusion.13
  1545.9 13.2 convert_reduce_fusion.1
  1559.3 9.1 multiply_reduce_fusion.2
  1569.2 4.4 fusion.54
  1573.6 4.3 fusion.53
  1578.4 15.1 convolution_bitcast_fusion.1
  1593.5 5.3 convolution_bitcast_fusion.4
  1598.8 9.8 convolution_bitcast_fusion.3
  1608.6 4.7 fusion.56
  1614.0 24.1 %all-reduce.1 = (f32[6,288]{1,0:T(8,128)}, f32[2,288]{1,0:T(2,128)}, f32[1152]{0:T(1024)}, f32[1152]{0:T(1024)}, f32[1152]{0:T(1024)}) all-reduce(f32[6,288]{1,0:T(8,128)S(1)} %convert_reduce_fusion.6, f32[2,288]{1,0:T(2,128)S(1)} %pad_maximum_fusion.3, f32[1152]{0:T(1024)S(1)} %copy-done.42, ...), channel_id=1, replica_groups=mesh['dp'=8,'tensor'=4] {'dp'}, use_global_device_ids=true, to_apply=%region_25.26 | all-reduce | flops 5760 | bytes 46080 | tf_op jit(solution)/shard_map/psum | solution.py:188
  1638.2 128.6 %all-reduce.14.cloned.1.call-done = (f32[1000,1152]{1,0:T(8,128)}, f32[1001,1152]{1,0:T(8,128)}) async-done(((f32[1000,1152]{1,0:T(8,128)}, f32[1001,1152]{1,0:T(8,128)}), (f32[1000,1152]{1,0:T(8,128)}, f32[1001,1152]{1,0:T(8,128)})) %all-reduce.14.cloned.1.call-update) | async-done | bytes 9220624 | tf_op jit(solution)/shard_map/psum | solution.py:205
  1766.7 300.5 %all-reduce.16.cloned.1.call-done = (f32[1152,6,288]{0,2,1:T(8,128)}, f32[1152,3,288]{0,2,1:T(8,128)}, f32[288,1152]{1,0:T(8,128)}, f32[1152,1152]{1,0:T(8,128)}, f32[1152,1152]{1,0:T(8,128)}) async-done(((f32[1152,6,288]{0,2,1:T(8,128)}, f32[1152,3,288]{0,2,1:T(8,128)}, f32[288,1152]{1,0:T(8,128)}, f32[1152,1152]{1,0:T(8,128)}, f32[1152,1152]{1,0:T(8,128)}), (f32[1152,6,288]{0,2,1:T(8,128)}, ...) | async-done | bytes 23887888 | tf_op jit(solution)/shard_map/psum | solution.py:188
  2067.2 5.1 copy.107
  2076.8 4.0 copy.109
  (231 shorter events, 78.9 us)
Async XLA Ops:
  7.2 509.5 %copy-start = (bf16[1152,1152]{1,0:T(8,128)(2,1)S(1)}, bf16[1152,1152]{1,0:T(8,128)(2,1)}, u32[]{:S(2)}) copy-start(bf16[1152,1152]{1,0:T(8,128)(2,1)} %param.32) | copy-start | bytes 7962628
  7.2 483.1 %all-reduce.10.cloned.1.call-start = ((), (), s32[]{:S(2)}) async-start(), calls=%async_computation | async-start | bytes 18874368 | tf_op jit(solution)/shard_map/psum | solution.py:100
  7.3 9.4 copy-start.6
  10.5 128.8 %copy-start.32 = (f32[8,256]{1,0:T(8,128)}, f32[8,256]{1,0:T(8,128)S(1)}, u32[]{:S(2)}) copy-start(f32[8,256]{1,0:T(8,128)S(1)} %broadcast_multiply_fusion.5) | copy-start | bytes 24580
  15.0 124.3 %copy-start.34 = (f32[8,256]{1,0:T(8,128)}, f32[8,256]{1,0:T(8,128)S(1)}, u32[]{:S(2)}) copy-start(f32[8,256]{1,0:T(8,128)S(1)} %add_rsqrt_fusion.1) | copy-start | bytes 24580
  135.9 11.2 copy-start.38
  165.0 700.2 %all-reduce.12.cloned.1.call-start = ((), (), s32[]{:S(2)}) async-start(), calls=%async_computation.1 | async-start | bytes 18874368 | tf_op jit(solution)/shard_map/psum | solution.py:125
  165.7 324.6 %copy-start.36 = (f32[1152]{0:T(1024)}, f32[1152]{0:T(1024)S(1)}, u32[]{:S(2)}) copy-start(f32[1152]{0:T(1024)S(1)} %convert_element_type.142) | copy-start | bytes 13828
  180.0 336.7 %copy-start.54 = (f32[8]{0:T(128)}, f32[8]{0:T(128)S(1)}, u32[]{:S(2)}) copy-start(f32[8]{0:T(128)S(1)} %compare_convert_fusion) | copy-start | bytes 100
  490.3 15.3 copy-start.57
  500.7 15.9 slice-start.10
  507.1 9.6 slice-start.11
  541.5 995.5 %all-reduce.18.cloned.1.call-start = ((), (), s32[]{:S(2)}) async-start(), calls=%async_computation.4 | async-start | bytes 37748736 | tf_op jit(solution)/shard_map/psum | solution.py:110
  555.3 318.4 %copy-start.55 = (f32[8]{0:T(128)S(1)}, f32[8]{0:T(128)}, u32[]{:S(2)}) copy-start(f32[8]{0:T(128)} %copy-done.54) | copy-start | bytes 100
  908.4 858.3 %all-reduce.14.cloned.1.call-start = ((), (), s32[]{:S(2)}) async-start(), calls=%async_computation.2 | async-start | bytes 18505728 | tf_op jit(solution)/shard_map/psum | solution.py:205
  909.1 627.9 %copy-start.29 = (f32[8,1152]{1,0:T(8,128)S(1)}, f32[8,1152]{1,0:T(8,128)}, u32[]{:S(2)}) copy-start(f32[8,1152]{1,0:T(8,128)} %copy-done.28) | copy-start | bytes 110596
  909.1 627.9 %copy-start.33 = (f32[8,256]{1,0:T(8,128)S(1)}, f32[8,256]{1,0:T(8,128)}, u32[]{:S(2)}) copy-start(f32[8,256]{1,0:T(8,128)} %copy-done.32) | copy-start | bytes 24580
  909.1 627.9 %copy-start.35 = (f32[8,256]{1,0:T(8,128)S(1)}, f32[8,256]{1,0:T(8,128)}, u32[]{:S(2)}) copy-start(f32[8,256]{1,0:T(8,128)} %copy-done.34) | copy-start | bytes 24580
  1537.0 22.2 %slice-start.2 = ((s8[4718592]{0:T(1024)(128)(4,1)}), s8[4194304]{0:T(1024)(128)(4,1)S(1)}, s32[]{:S(2)}) async-start(s8[4718592]{0:T(1024)(128)(4,1)} %bitcast.124), calls=%async_computation.7 | async-start | bytes 8388608
  1537.0 22.2 %slice-start.4 = ((s8[9437184]{0:T(1024)(128)(4,1)}), s8[4194304]{0:T(1024)(128)(4,1)S(1)}, s32[]{:S(2)}) async-start(s8[9437184]{0:T(1024)(128)(4,1)} %bitcast.126), calls=%async_computation.9 | async-start | bytes 8388608
  1537.0 22.2 %slice-start.5 = ((s8[9437184]{0:T(1024)(128)(4,1)}), s8[4194304]{0:T(1024)(128)(4,1)S(1)}, s32[]{:S(2)}) async-start(s8[9437184]{0:T(1024)(128)(4,1)} %bitcast.126), calls=%async_computation.10 | async-start | bytes 8388608
  1537.0 22.2 %slice-start.7 = ((s8[9437184]{0:T(1024)(128)(4,1)}), s8[4194304]{0:T(1024)(128)(4,1)S(1)}, s32[]{:S(2)}) async-start(s8[9437184]{0:T(1024)(128)(4,1)} %bitcast.128), calls=%async_computation.12 | async-start | bytes 8388608
  1537.0 22.2 %slice-start.8 = ((s8[9437184]{0:T(1024)(128)(4,1)}), s8[4194304]{0:T(1024)(128)(4,1)S(1)}, s32[]{:S(2)}) async-start(s8[9437184]{0:T(1024)(128)(4,1)} %bitcast.128), calls=%async_computation.13 | async-start | bytes 8388608
  1545.9 13.3 slice-start.3
  1545.9 13.3 slice-start.6
  1545.9 13.3 slice-start.9
  1545.9 13.3 copy-start.37
  1559.3 9.9 copy-start.51
  1569.2 9.2 copy-start.41
  1577.9 15.6 copy-start.18
  1577.9 489.3 %all-reduce.16.cloned.1.call-start = ((), (), s32[]{:S(2)}) async-start(), calls=%async_computation.3 | async-start | bytes 47775744 | tf_op jit(solution)/shard_map/psum | solution.py:188
  2072.3 12.5 slice-start.16
  (51 other events, 257.0 us)
Sparse Core Ops, SparseCore 0:
  165.1 325.1 all-reduce.9
  541.6 323.5 all-reduce.11
  908.5 628.3 all-reduce.17
  1578.0 188.6 all-reduce.13
  1772.5 294.6 all-reduce.15
where the time goes:
time: 2100 us
  waiting for transfers between devices  1660 us (79%)
  matrix products  144 us (7%)
  blocking collectives  115 us (5%)
  local copies, waits for them, and re-layouts  84.7 us (4%)
  other arithmetic  78.3 us (4%)
    psum x1, waiting for transfers between devices, local(): branch = lax.psum(mlp_part, 'tensor') + down_bias.astype(wide)  611 us
    psum x1, waiting for transfers between devices, local(): attention = lax.psum(attn_part, 'tensor') + proj_bias.astype(wide)  310 us
    psum x1, waiting for transfers between devices, local(): d_hidden_mlp = lax.psum(d_mlp_part, 'tensor')  310 us
    psum x1, waiting for transfers between devices, local(): lax.psum((grad_qkv_weight, grad_qv_bias, grad_proj_weight, grad_proj_bias...  300 us
    psum x1, waiting for transfers between devices, local(): lax.psum((grad_time_table, grad_class_table), ('dp', 'tensor'))  129 us
    all_gather x1, blocking collectives, local(): modulation = lax.all_gather(mod_local, 'tensor', axis=2, tiled=True)  91.1 us
    unnamed x174, local copies, waits for them, and re-layouts  57 us
  transfers between devices with their start and end apart: 5, of which 5 were waited for; matrix products, arithmetic and copies ran while one was open for 4% of the time, Pallas kernels for 0%

commit v1 on v0

--- a/solution.py
+++ b/solution.py
@@ -122,7 +122,7 @@
         (grad_down_weight, grad_down_bias, grad_up_weight, grad_up_bias), "dp"
     )
     d_mlp_part = jnp.einsum("gsf,df->gsd", d_pre, up_weight, preferred_element_type=wide)
-    d_hidden_mlp = lax.psum(d_mlp_part, "tensor")
+    d_hidden_mlp = jnp.sum(lax.all_gather(d_mlp_part, "tensor"), axis=0)
     d_shift_mlp = jnp.sum(d_hidden_mlp, axis=1)
     d_scale_mlp = jnp.sum(d_hidden_mlp * normed_mlp, axis=1)
     d_middle = grad_out + norm_back(d_hidden_mlp * (1.0 + scale_mlp), normed_mlp, inverse_mlp)

time: 2100 us -> 2430 us (1.16)
  waiting for transfers between devices: 1660 us -> 1950 us
  other arithmetic: 78.3 us -> 109 us
    all_gather x0 -> x1, waiting for transfers between devices: none -> 616 us  [local(): d_hidden_mlp = jnp.sum(lax.all_gather(d_mlp_part, 'tensor'), axis=0)]
    psum x1 -> x0, waiting for transfers between devices: 310 us -> none  [local(): d_hidden_mlp = lax.psum(d_mlp_part, 'tensor')]
    reduce_sum x0 -> x3, other arithmetic: none -> 31 us  [the longest x1 17.6 us: local(): d_hidden_mlp = jnp.sum(lax.all_gather(d_mlp_part, 'tensor'), axis=0)]
    unnamed x174 -> x176, local copies, waits for them, and re-layouts: 57 us -> 57.3 us
where the time goes in v1:
time: 2430 us; the launch traced here: 2420 us
  waiting for transfers between devices  1950 us (80%)
  matrix products  145 us (6%)
  blocking collectives  115 us (5%)
  other arithmetic  109 us (4%)
  local copies, waits for them, and re-layouts  85 us (3%)
    all_gather x1, waiting for transfers between devices, local(): d_hidden_mlp = jnp.sum(lax.all_gather(d_mlp_part, 'tensor'), axis=0)  616 us
    psum x1, waiting for transfers between devices, local(): branch = lax.psum(mlp_part, 'tensor') + down_bias.astype(wide)  597 us
    psum x1, waiting for transfers between devices, local(): attention = lax.psum(attn_part, 'tensor') + proj_bias.astype(wide)  310 us
    psum x1, waiting for transfers between devices, local(): lax.psum((grad_qkv_weight, grad_qv_bias, grad_proj_weight, grad_proj_bias...  300 us
    psum x1, waiting for transfers between devices, local(): lax.psum((grad_time_table, grad_class_table), ('dp', 'tensor'))  128 us
    all_gather x1, blocking collectives, local(): modulation = lax.all_gather(mod_local, 'tensor', axis=2, tiled=True)  90.7 us
    unnamed x176, local copies, waits for them, and re-layouts  57.3 us
  transfers between devices with their start and end apart: 5, of which 5 were waited for; matrix products, arithmetic and copies ran while one was open for 4% of the time, Pallas kernels for 0%

profile of v1, /device:TPU:0, one launch (start us, length us, event | category | flops | bytes accessed | tf_op | source)
XLA Modules:
  0.0 2422.9 jit_solution(9778393584793108920)
XLA Ops:
  10.5 4.5 fusion.14
  19.4 90.7 %all_gather.9 = f32[8,6,1152]{1,0,2:T(8,128)} all-gather(f32[8,6,288]{1,0,2:T(8,128)} %copy.75), channel_id=1, replica_groups=mesh['dp'=8,'tensor'=4] {'tensor'}, dimensions={2}, use_global_device_ids=true | all-gather | bytes 276480 | tf_op jit(solution)/shard_map/all_gather | solution.py:73
  110.1 22.0 fusion.73
  138.9 7.8 fusion.40
  159.1 5.6 fusion.49
  179.8 310.3 %all-reduce.9.cloned.1.call-done = f32[8,256,1152]{2,1,0:T(8,128)} async-done(((f32[8,256,1152]{2,1,0:T(8,128)}), f32[8,256,1152]{2,1,0:T(8,128)}) %all-reduce.9.cloned.1.call-update) | async-done | bytes 9437200 | tf_op jit(solution)/shard_map/psum | solution.py:100
  490.1 10.4 fusion.71
  500.5 4.9 multiply_reduce_fusion.4
  506.8 9.6 fusion.35
  516.5 12.8 convert_reduce_fusion.2
  531.4 9.4 fusion.33
  541.6 13.9 fusion.31
  555.5 615.9 %all-gather.3.cloned.1.call-done = f32[32,256,1152]{2,1,0:T(8,128)} async-done(((f32[8,256,1152]{2,1,0:T(8,128)}), f32[32,256,1152]{2,1,0:T(8,128)}) %all-gather.3.cloned.1.call-update) | async-done | bytes 37748752 | tf_op jit(solution)/shard_map/all_gather | solution.py:125
  1171.4 17.6 reduce_sum.212
  1188.9 8.3 multiply_reduce_fusion.1
  1198.1 11.5 convert_reduce_fusion.3
  1225.2 8.0 convolution_bitcast_fusion.2
  1233.8 16.6 convolution_bitcast_fusion
  1250.4 13.4 reduce.1
  1263.9 597.4 %all-reduce.15.cloned.1.call-done = (f32[8,256,1152]{2,1,0:T(8,128)}, f32[8,256,1152]{2,1,0:T(8,128)}) async-done(((f32[8,256,1152]{2,1,0:T(8,128)}, f32[8,256,1152]{2,1,0:T(8,128)}), (f32[8,256,1152]{2,1,0:T(8,128)}, f32[8,256,1152]{2,1,0:T(8,128)})) %all-reduce.15.cloned.1.call-update) | async-done | bytes 18874384 | tf_op jit(solution)/shard_map/psum | solution.py:110
  1861.4 8.6 fusion.13
  1870.0 13.2 convert_reduce_fusion.1
  1883.4 9.1 multiply_reduce_fusion.2
  1893.3 4.4 fusion.54
  1902.3 15.0 convolution_bitcast_fusion.1
  1917.4 5.3 convolution_bitcast_fusion.4
  1922.7 9.9 convolution_bitcast_fusion.3
  1932.6 4.7 fusion.56
  1938.3 24.2 %all-reduce.1 = (f32[6,288]{1,0:T(8,128)}, f32[2,288]{1,0:T(2,128)}, f32[1152]{0:T(1024)}, f32[1152]{0:T(1024)}, f32[1152]{0:T(1024)}) all-reduce(f32[6,288]{1,0:T(8,128)S(1)} %convert_reduce_fusion.6, f32[2,288]{1,0:T(2,128)S(1)} %pad_maximum_fusion.3, f32[1152]{0:T(1024)S(1)} %copy-done.42, ...), channel_id=1, replica_groups=mesh['dp'=8,'tensor'=4] {'dp'}, use_global_device_ids=true, to_apply=%region_25.26 | all-reduce | flops 5760 | bytes 46080 | tf_op jit(solution)/shard_map/psum | solution.py:188
  1962.5 128.3 %all-reduce.11.cloned.1.call-done = (f32[1000,1152]{1,0:T(8,128)}, f32[1001,1152]{1,0:T(8,128)}) async-done(((f32[1000,1152]{1,0:T(8,128)}, f32[1001,1152]{1,0:T(8,128)}), (f32[1000,1152]{1,0:T(8,128)}, f32[1001,1152]{1,0:T(8,128)})) %all-reduce.11.cloned.1.call-update) | async-done | bytes 9220624 | tf_op jit(solution)/shard_map/psum | solution.py:205
  2090.9 300.5 %all-reduce.13.cloned.1.call-done = (f32[1152,6,288]{0,2,1:T(8,128)}, f32[1152,3,288]{0,2,1:T(8,128)}, f32[288,1152]{1,0:T(8,128)}, f32[1152,1152]{1,0:T(8,128)}, f32[1152,1152]{1,0:T(8,128)}) async-done(((f32[1152,6,288]{0,2,1:T(8,128)}, f32[1152,3,288]{0,2,1:T(8,128)}, f32[288,1152]{1,0:T(8,128)}, f32[1152,1152]{1,0:T(8,128)}, f32[1152,1152]{1,0:T(8,128)}), (f32[1152,6,288]{0,2,1:T(8,128)}, ...) | async-done | bytes 23887888 | tf_op jit(solution)/shard_map/psum | solution.py:188
  2391.3 5.1 copy.123
  (236 shorter events, 88.1 us)
Async XLA Ops:
  7.2 509.3 %copy-start = (bf16[1152,1152]{1,0:T(8,128)(2,1)S(1)}, bf16[1152,1152]{1,0:T(8,128)(2,1)}, u32[]{:S(2)}) copy-start(bf16[1152,1152]{1,0:T(8,128)(2,1)} %param.32) | copy-start | bytes 7962628
  7.2 482.9 %all-reduce.9.cloned.1.call-start = ((), (), s32[]{:S(2)}) async-start(), calls=%async_computation | async-start | bytes 18874368 | tf_op jit(solution)/shard_map/psum | solution.py:100
  7.3 9.3 copy-start.6
  10.5 128.3 %copy-start.32 = (f32[8,256]{1,0:T(8,128)}, f32[8,256]{1,0:T(8,128)S(1)}, u32[]{:S(2)}) copy-start(f32[8,256]{1,0:T(8,128)S(1)} %broadcast_multiply_fusion.5) | copy-start | bytes 24580
  15.0 123.8 %copy-start.34 = (f32[8,256]{1,0:T(8,128)}, f32[8,256]{1,0:T(8,128)S(1)}, u32[]{:S(2)}) copy-start(f32[8,256]{1,0:T(8,128)S(1)} %add_rsqrt_fusion.1) | copy-start | bytes 24580
  135.5 11.2 copy-start.38
  164.8 1006.6 %all-gather.3.cloned.1.call-start = ((), (), s32[]{:S(2)}) async-start(), calls=%async_computation.1 | async-start | bytes 47185920 | tf_op jit(solution)/shard_map/all_gather | solution.py:125
  165.5 324.6 %copy-start.36 = (f32[1152]{0:T(1024)}, f32[1152]{0:T(1024)S(1)}, u32[]{:S(2)}) copy-start(f32[1152]{0:T(1024)S(1)} %convert_element_type.142) | copy-start | bytes 13828
  179.7 336.7 %copy-start.55 = (f32[8]{0:T(128)}, f32[8]{0:T(128)S(1)}, u32[]{:S(2)}) copy-start(f32[8]{0:T(128)S(1)} %compare_convert_fusion) | copy-start | bytes 100
  490.1 15.3 copy-start.58
  500.5 16.0 slice-start.10
  506.8 9.6 slice-start.11
  540.8 1320.5 %all-reduce.15.cloned.1.call-start = ((), (), s32[]{:S(2)}) async-start(), calls=%async_computation.4 | async-start | bytes 37748736 | tf_op jit(solution)/shard_map/psum | solution.py:110
  1233.1 857.7 %all-reduce.11.cloned.1.call-start = ((), (), s32[]{:S(2)}) async-start(), calls=%async_computation.2 | async-start | bytes 18505728 | tf_op jit(solution)/shard_map/psum | solution.py:205
  1250.4 610.9 %copy-start.29 = (f32[8,1152]{1,0:T(8,128)S(1)}, f32[8,1152]{1,0:T(8,128)}, u32[]{:S(2)}) copy-start(f32[8,1152]{1,0:T(8,128)} %copy-done.28) | copy-start | bytes 110596
  1250.4 610.9 %copy-start.33 = (f32[8,256]{1,0:T(8,128)S(1)}, f32[8,256]{1,0:T(8,128)}, u32[]{:S(2)}) copy-start(f32[8,256]{1,0:T(8,128)} %copy-done.32) | copy-start | bytes 24580
  1250.4 610.9 %copy-start.35 = (f32[8,256]{1,0:T(8,128)S(1)}, f32[8,256]{1,0:T(8,128)}, u32[]{:S(2)}) copy-start(f32[8,256]{1,0:T(8,128)} %copy-done.34) | copy-start | bytes 24580
  1861.3 22.0 slice-start.2
  1861.3 22.0 slice-start.4
  1861.3 22.0 slice-start.5
  1861.3 22.0 slice-start.7
  1861.3 22.0 slice-start.8
  1870.0 13.3 slice-start.3
  1870.0 13.3 slice-start.6
  1870.0 13.3 slice-start.9
  1870.0 13.3 copy-start.37
  1883.4 9.2 copy-start.7
  1883.4 9.2 copy-start.27
  1883.4 9.9 copy-start.52
  1902.1 15.3 copy-start.18
  1902.1 489.3 %all-reduce.13.cloned.1.call-start = ((), (), s32[]{:S(2)}) async-start(), calls=%async_computation.3 | async-start | bytes 47775744 | tf_op jit(solution)/shard_map/psum | solution.py:188
  2396.5 12.5 slice-start.16
  (52 other events, 252.6 us)
Sparse Core Ops, SparseCore 0:
  164.9 325.1 all-reduce.8
  540.9 630.3 all-gather.2
  1233.3 627.9 all-reduce.14
  1902.2 188.6 all-reduce.10
  2096.6 294.6 all-reduce.12
